TPU v7x, 256 devices: a whole 4x4x8 slice. The times are simulated.
256 devices in a mesh: comp: 4 (over y), gx: 8 (over x, z_lo), gy: 8 (over z_hi, core).
Axes of the slice: x: 4, y: 4, z: 8 (z_hi: 4, z_lo: 2; z = z_hi * 2 + z_lo), core: 2. Of those that a mesh axis runs over, the one named last changes fastest.
Arguments:
- zonal_flow_speed: float32 [64, 128, 1024], P('comp', 'gx', 'gy'), may hold values from -5 to 5
- meridional_flow_speed: float32 [64, 128, 1024], P('comp', 'gx', 'gy'), may hold values from -5 to 5
- thermal_anomaly: float32 [64, 128, 1024], P('comp', 'gx', 'gy'), may hold values from -6 to 6
- brine_anomaly_values: float32 [64, 128, 1024], P('comp', 'gx', 'gy'), may hold values from -6 to 6
- marine_indicator: int32 [128, 1024], P('gx', 'gy'), may hold values 0 or 1
- seafloor_layer: int32 [128, 1024], P('gx', 'gy'), may hold values from 1 to 64
- dissolved_species: float32 [24, 64, 8, 4, 4, 1024], P(None, None, 'gx', 'comp', None, 'gy'), may hold values from 0.05 to 2
- topmost_sunshine: float32 [8, 4, 4, 1024], P('gx', 'comp', None, 'gy'), may hold values from 0.3 to 3
- attenuation_coefficient: float32 [24], replicated, may hold values from 0.01 to 0.1
- peak_intake_speed: float32 [24], replicated, may hold values from 0.2 to 2
- feedstock_midpoint_constant: float32 [24], replicated, may hold values from 0.05 to 1
- photon_midpoint_constant: float32 [24], replicated, may hold values from 0.05 to 1
- stoichiometry_matrix: float32 [24, 24], replicated, may hold values from -1.25 to 1.25
Outputs:
- east_new: float32 [64, 128, 1024], P('comp', 'gx', 'gy')
- north_new: float32 [64, 128, 1024], P('comp', 'gx', 'gy')
- warmed_result: float32 [64, 128, 1024], P('comp', 'gx', 'gy')
- salt_mixed: float32 [64, 128, 1024], P('comp', 'gx', 'gy')
- buoyancy: float32 [64, 128, 1024], P('comp', 'gx', 'gy')
- result: float32 [24, 64, 8, 4, 4, 1024], P(None, None, 'gx', 'comp', None, 'gy')
All inputs are finite; a program needn't handle non-finite values. No bound on the sum of `marine_indicator` on one device may be relied on, other than what follows from the above.
Results may differ from a plain program's by a relative error of at most 0.00007.
Values sent between devices are 32-bit elements; how exact they have to be, the bound alone decides.
A program may use at most 128 MiB of HBM per device.

v0:
```python
import jax
import jax.numpy as jnp
from jax import lax
from jax.sharding import PartitionSpec as P

NSUB = 2
DT_FLOW = 0.1
CORIOLIS = 0.3
MIXING = 0.15
COURANT = 0.24
DT_BIO = 0.5
WARMING_FACTOR = 0.5
CLEAR_WATER = 0.5
HIGHEST = lax.Precision.HIGHEST


def padded(x, sides, width):
    edges = {}
    for axis, dim in sides:
        count, length = (lax.axis_size(axis), x.shape[dim])
        up = [(i, (i + 1) % count) for i in range(count - 1)]
        last = lax.slice_in_dim(x, length - width, length, axis=dim)
        first = lax.slice_in_dim(x, 0, width, axis=dim)
        edges[dim] = (
            lax.ppermute(last, axis, up),
            lax.ppermute(first, axis, [(b, a) for a, b in up]),
        )
    done = []
    for _, dim in sides:
        low, high = edges[dim]
        around = [(width, width) if d in done else (0, 0) for d in range(x.ndim)]
        x = jnp.concatenate([jnp.pad(low, around), x, jnp.pad(high, around)], axis=dim)
        done.append(dim)
    return x


def from_everyone(x, axis):
    copies = jnp.broadcast_to(x, (lax.axis_size(axis), *x.shape))
    return lax.all_to_all(copies, axis, split_axis=0, concat_axis=0, tiled=True)


def in_order(pieces, dim):
    dims = list(pieces.shape[1:])
    dims[dim] *= pieces.shape[0]
    return jnp.moveaxis(pieces, 0, dim).reshape(dims)


def collect(x, axis, dim):
    pieces = from_everyone(x, axis)
    return in_order(pieces, dim)


def from_behind(x, axis, by):
    count = lax.axis_size(axis)
    pairs = [(i, i + by) for i in range(count) if 0 <= i + by < count]
    return lax.ppermute(x, axis, pairs)


def passed_along(x, axis, by):
    count = lax.axis_size(axis)
    return lax.ppermute(x, axis, [(i, (i + by) % count) for i in range(count)])


def extended_2(cells, sides, width):
    for axis, dim in sides:
        count = lax.axis_size(axis)
        ends = count - 1
        head = lax.slice_in_dim(cells, 0, width, axis=dim)
        tail = lax.slice_in_dim(cells, cells.shape[dim] - width, cells.shape[dim], axis=dim)
        cells = jnp.concatenate(
            [
                lax.ppermute(tail, axis, [(i, (i + 1) % count) for i in range(ends)]),
                cells,
                lax.ppermute(head, axis, [((i + 1) % count, i) for i in range(ends)]),
            ],
            axis=dim,
        )
    return cells


def on_device(
    zonal_flow_speed,
    meridional_flow_speed,
    thermal_anomaly,
    brine_anomaly_values,
    marine_indicator,
    seafloor_layer,
    dissolved_species,
    topmost_sunshine,
    attenuation_coefficient,
    peak_intake_speed,
    feedstock_midpoint_constant,
    photon_midpoint_constant,
    stoichiometry_matrix,
):
    group_index = lax.axis_index("comp")
    group_count = lax.axis_size("comp")
    levels_dev, tile_rows, tile_cols = zonal_flow_speed.shape
    tracer_count = dissolved_species.shape[0]
    level_count = dissolved_species.shape[1]
    sub_rows = dissolved_species.shape[4]
    rimmed = padded(jnp.stack([marine_indicator, seafloor_layer]), (("gx", 1), ("gy", 2)), 1)
    depth_index = group_index * levels_dev + jnp.arange(levels_dev, dtype=jnp.int32)[:, None, None]
    wet_rimmed = ((rimmed[0][None] == 1) & (depth_index < rimmed[1][None])).astype(jnp.float32)
    submerged_indicator = wet_rimmed[:, 1:-1, 1:-1]
    face_east = wet_rimmed[:, :-1, 1:-1] * wet_rimmed[:, 1:, 1:-1]
    face_north = wet_rimmed[:, 1:-1, :-1] * wet_rimmed[:, 1:-1, 1:]
    open_east = face_east[:, 1:]
    open_north = face_north[:, :, 1:]
    seawater_heaviness = submerged_indicator * (-0.2 * thermal_anomaly + 0.8 * brine_anomaly_values)
    column_total = jnp.sum(seawater_heaviness, axis=0)
    totals = collect(column_total[None], "comp", 0)
    earlier_groups = (jnp.arange(group_count, dtype=jnp.int32) < group_index).astype(jnp.float32)
    offset = jnp.sum(totals * earlier_groups[:, None, None], axis=0)
    strict_lower = (jnp.arange(levels_dev)[:, None] > jnp.arange(levels_dev)[None, :]).astype(
        jnp.float32
    )
    depth_above = offset[None] + jnp.dot(
        strict_lower, seawater_heaviness.reshape(levels_dev, -1), precision=HIGHEST
    ).reshape(seawater_heaviness.shape)
    weight_of_overlying = depth_above + 0.5 * seawater_heaviness
    padded_field = padded(
        jnp.stack([thermal_anomaly, brine_anomaly_values, weight_of_overlying]),
        (("gx", 2), ("gy", 3)),
        1,
    )
    pressure_east = padded_field[2, :, 2:, 1:-1]
    pressure_north = padded_field[2, :, 1:-1, 2:]
    east_new = open_east * (
        zonal_flow_speed
        + DT_FLOW * (CORIOLIS * meridional_flow_speed - (pressure_east - weight_of_overlying))
    )
    north_new = open_north * (
        meridional_flow_speed
        + DT_FLOW * (-CORIOLIS * zonal_flow_speed - (pressure_north - weight_of_overlying))
    )
    east_column, north_column = (
        lax.all_to_all(east_new, "comp", split_axis=1, concat_axis=0, tiled=True),
        lax.all_to_all(north_new, "comp", split_axis=1, concat_axis=0, tiled=True),
    )
    scalar_pair = padded_field[:2]
    flux_east = face_east[None] * (scalar_pair[:, :, 1:, 1:-1] - scalar_pair[:, :, :-1, 1:-1])
    flux_north = face_north[None] * (scalar_pair[:, :, 1:-1, 1:] - scalar_pair[:, :, 1:-1, :-1])
    blended_couple = scalar_pair[:, :, 1:-1, 1:-1] + MIXING * (
        flux_east[:, :, 1:]
        - flux_east[:, :, :-1]
        + (flux_north[:, :, :, 1:] - flux_north[:, :, :, :-1])
    )
    thermal_blended = blended_couple[0]
    salt_mixed = blended_couple[1]
    courant_east = COURANT * jnp.tanh(east_column)
    courant_north = COURANT * jnp.tanh(north_column)
    row_start = group_index * sub_rows
    sea_rows = lax.dynamic_slice_in_dim(marine_indicator, row_start, sub_rows, 0)
    bottom_rows = lax.dynamic_slice_in_dim(seafloor_layer, row_start, sub_rows, 0)
    column_depth = jnp.arange(level_count, dtype=jnp.int32)[:, None, None]
    wet_column = ((sea_rows[None] == 1) & (column_depth < bottom_rows[None])).astype(jnp.float32)
    north_before = from_behind(courant_north[:, :, -1], "gy", 1)
    courant_faces = jnp.concatenate([north_before[:, :, None], courant_north], axis=2)

    def neighbour_row(edge_row, shift_by, edge_group):
        within = passed_along(edge_row, "comp", shift_by)
        across = from_behind(within, "gx", shift_by)
        return jnp.where(group_index == edge_group, across, within)

    tracer_field = dissolved_species.reshape(tracer_count, level_count, sub_rows, tile_cols)
    east_below = neighbour_row(courant_east[:, -1], 1, 0)
    east_faces = jnp.concatenate([east_below[:, None], courant_east], axis=1)
    for substep in range(NSUB):
        row_below = neighbour_row(tracer_field[:, :, -1], 1, 0)
        beyond = neighbour_row(tracer_field[:, :, 0], -1, group_count - 1)
        extended = jnp.concatenate(
            [row_below[:, :, None], tracer_field, beyond[:, :, None]], axis=2
        )
        flux_faces = (
            jnp.maximum(east_faces, 0.0) * extended[:, :, :-1]
            + jnp.minimum(east_faces, 0.0) * extended[:, :, 1:]
        )
        change_east = flux_faces[:, :, 1:] - flux_faces[:, :, :-1]
        north_field = extended_2(tracer_field, (("gy", 3),), 1)
        flux_column = (
            jnp.maximum(courant_faces, 0.0) * north_field[:, :, :, :-1]
            + jnp.minimum(courant_faces, 0.0) * north_field[:, :, :, 1:]
        )
        change_north = flux_column[:, :, :, 1:] - flux_column[:, :, :, :-1]
        tracer_field = wet_column * (tracer_field - change_east - change_north)
    layer_depth = 2.0 / level_count
    optical_step = layer_depth * (
        CLEAR_WATER
        + jnp.tensordot(attenuation_coefficient, tracer_field, axes=1, precision=HIGHEST)
    )
    strict_column = (jnp.arange(level_count)[:, None] > jnp.arange(level_count)[None, :]).astype(
        jnp.float32
    )
    optical_above = jnp.dot(
        strict_column, optical_step.reshape(level_count, -1), precision=HIGHEST
    ).reshape(optical_step.shape)
    transmitted = jnp.exp(-optical_above)
    surface = topmost_sunshine.reshape(sub_rows, tile_cols)[None]
    light_level = surface * transmitted * jnp.exp(-0.5 * optical_step)
    warming_step = wet_column * surface * transmitted * (1.0 - jnp.exp(-optical_step)) / layer_depth
    warming_reverse = lax.all_to_all(warming_step, "comp", split_axis=0, concat_axis=1, tiled=True)
    nutrient = tracer_field[0]
    uptake_rates = (
        peak_intake_speed[:, None, None, None]
        * (nutrient / (feedstock_midpoint_constant[:, None, None, None] + nutrient))
        * (light_level / (light_level + photon_midpoint_constant[:, None, None, None]))
        * tracer_field
    )
    change = jnp.tensordot(stoichiometry_matrix, uptake_rates, axes=1, precision=HIGHEST)
    result = tracer_field + DT_BIO * wet_column * change
    warmed_result = thermal_blended + WARMING_FACTOR * warming_reverse
    buoyancy = submerged_indicator * (0.2 * warmed_result - 0.8 * salt_mixed)
    return (
        east_new,
        north_new,
        warmed_result,
        salt_mixed,
        buoyancy,
        result.reshape(dissolved_species.shape),
    )


def solution(mesh):
    return jax.shard_map(
        on_device,
        mesh=mesh,
        in_specs=(
            P("comp", "gx", "gy"),
            P("comp", "gx", "gy"),
            P("comp", "gx", "gy"),
            P("comp", "gx", "gy"),
            P("gx", "gy"),
            P("gx", "gy"),
            P(None, None, "gx", "comp", None, "gy"),
            P("gx", "comp", None, "gy"),
            P(),
            P(),
            P(),
            P(),
            P(),
        ),
        out_specs=(
            P("comp", "gx", "gy"),
            P("comp", "gx", "gy"),
            P("comp", "gx", "gy"),
            P("comp", "gx", "gy"),
            P("comp", "gx", "gy"),
            P(None, None, "gx", "comp", None, "gy"),
        ),
        check_vma=False,
    )
```

profile of v0, /device:TPU:15, one launch (start us, length us, event | category | flops | bytes accessed | tf_op | source)
XLA Modules:
  0.0 252.4 jit_solution(14438228290551515185)
XLA Ops:
  1.5 2.6 %collective-permute-start.3 = (s32[2,16,1]{2,1,0:T(8,128)S(1)}, s32[2,16,1]{2,1,0:T(8,128)S(1)}, u32[]{:S(2)}, u32[]{:S(2)}) collective-permute-start(s32[2,16,1]{2,1,0:T(8,128)S(1)} %get-tuple-element.73), channel_id=1, source_target_pairs={{1,0},{2,1},{3,2},{4,3},{5,4},{6,5},{7,6},{9,8},{10,9},{11,10},{12... | collective-permute-start | bytes 392 | tf_op jit(solution)/shard_map/ppermute | solution.py:26
  4.1 4.8 %collective-permute-start = (s32[2,16,1]{2,1,0:T(8,128)S(1)}, s32[2,16,1]{2,1,0:T(8,128)S(1)}, u32[]{:S(2)}, u32[]{:S(2)}) collective-permute-start(s32[2,16,1]{2,1,0:T(8,128)S(1)} %get-tuple-element.72), channel_id=1, source_target_pairs={{0,1},{1,2},{2,3},{3,4},{4,5},{5,6},{6,7},{8,9},{9,10},{10,11},{11... | collective-permute-start | bytes 392 | tf_op jit(solution)/shard_map/ppermute | solution.py:25
  9.6 3.8 %collective-permute-start.2 = (s32[2,1,128]{2,1,0:T(1,128)S(1)}, s32[2,1,128]{2,1,0:T(1,128)S(1)}, u32[]{:S(2)}, u32[]{:S(2)}) collective-permute-start(s32[2,1,128]{2,1,0:T(1,128)S(1)} %get-tuple-element.71), channel_id=1, source_target_pairs={{8,0},{16,8},{24,16},{32,24},{40,32},{48,40},{56,48},{9,1},{17,9},... | collective-permute-start | bytes 3080 | tf_op jit(solution)/shard_map/ppermute | solution.py:26
  13.4 1.9 collective-permute-start.1
  15.4 3.7 %copy.347 = f32[24,64,1,1,4,128]{5,0,1,4,3,2:T(8,128)S(1)} copy(f32[24,64,1,1,4,128]{5,4,3,2,1,0:T(4,128)} %param.19) | data formatting | bytes 6291456 | tf_op args[6]
  19.1 3.6 %fusion.72 = (f32[24,64,4,1]{3,0,1,2:T(8,128)}, f32[24,64,4,1]{3,0,1,2:T(8,128)}) fusion(f32[24,64,4,128]{3,0,1,2:T(8,128)S(1)} %bitcast.166), kind=kLoop, calls=%fused_computation.157 | loop fusion | bytes 98304 | tf_op jit(solution)/shard_map/slice | solution.py:69
  22.7 3.1 %copy.252 = f32[24,64,4,1]{1,0,3,2:T(8,128)} copy(f32[24,64,4,1]{3,0,1,2:T(8,128)} %get-tuple-element.54) | data formatting | bytes 49152 | tf_op jit(solution)/shard_map/slice | solution.py:69
  25.8 2.7 %collective-permute-start.15 = (f32[24,64,4,1]{1,0,3,2:T(8,128)}, f32[24,64,4,1]{1,0,3,2:T(8,128)}, u32[]{:S(2)}, u32[]{:S(2)}) collective-permute-start(f32[24,64,4,1]{1,0,3,2:T(8,128)} %copy.252), channel_id=1, source_target_pairs={{0,1},{1,2},{2,3},{3,4},{4,5},{5,6},{6,7},{8,9},{9,10},{10,11},{11... | collective-permute-start | bytes 73736 | tf_op jit(solution)/shard_map/ppermute | solution.py:72
  30.9 3.1 %copy.255 = f32[24,64,4,1]{1,0,3,2:T(8,128)} copy(f32[24,64,4,1]{3,0,1,2:T(8,128)} %get-tuple-element.55) | data formatting | bytes 49152 | tf_op jit(solution)/shard_map/slice | solution.py:68
  34.0 2.2 collective-permute-start.16
  37.2 1.7 fusion.70
  39.5 4.3 %all-to-all-start = ((f32[4,1,16,128]{3,2,1,0:T(8,128)}), f32[4,1,16,128]{3,2,1,0:T(8,128)S(1)}, u32[]{:S(2)}, u32[]{:S(2)}) async-start(f32[4,1,16,128]{3,2,1,0:T(8,128)} %broadcast_in_dim.10), calls=%async_computation | async-start | bytes 65536 | tf_op jit(solution)/shard_map/all_to_all | solution.py:39
  43.9 1.9 slice_multiply_fusion
  50.0 2.7 %collective-permute-start.6 = (f32[3,16,16,1]{3,1,2,0:T(8,128)S(1)}, f32[3,16,16,1]{3,1,2,0:T(8,128)S(1)}, u32[]{:S(2)}, u32[]{:S(2)}) collective-permute-start(f32[3,16,16,1]{3,1,2,0:T(8,128)S(1)} %get-tuple-element.57), channel_id=1, source_target_pairs={{1,0},{2,1},{3,2},{4,3},{5,4},{6,5},{7,6},{9,8},{10,9},{11,10},{12... | collective-permute-start | bytes 9224 | tf_op jit(solution)/shard_map/ppermute | solution.py:26
  52.7 4.3 %collective-permute-start.4 = (f32[3,16,1,128]{3,1,2,0:T(8,128)S(1)}, f32[3,16,1,128]{3,1,2,0:T(8,128)S(1)}, u32[]{:S(2)}, u32[]{:S(2)}) collective-permute-start(f32[3,16,1,128]{3,1,2,0:T(8,128)S(1)} %get-tuple-element.61), channel_id=1, source_target_pairs={{8,0},{16,8},{24,16},{32,24},{40,32},{48,40},{56,48},{9,1},{17,9},... | collective-permute-start | bytes 73736 | tf_op jit(solution)/shard_map/ppermute | solution.py:26
  57.0 1.9 collective-permute-start.5
  59.1 6.0 %collective-permute-done.6 = f32[3,16,16,1]{3,1,2,0:T(8,128)S(1)} collective-permute-done((f32[3,16,16,1]{3,1,2,0:T(8,128)S(1)}, f32[3,16,16,1]{3,1,2,0:T(8,128)S(1)}, u32[]{:S(2)}, u32[]{:S(2)}) %collective-permute-start.6) | collective-permute-done | bytes 3104 | tf_op jit(solution)/shard_map/ppermute | solution.py:26
  67.8 1.8 fusion.48
  69.6 5.4 %all-to-all-start.2 = ((f32[16,16,128]{2,0,1:T(8,128)}), f32[16,16,128]{2,0,1:T(8,128)}, u32[]{:S(2)}, u32[]{:S(2)}) async-start(f32[16,16,128]{2,0,1:T(8,128)} %get-tuple-element.58), calls=%async_computation.2 | async-start | bytes 262144 | tf_op jit(solution)/shard_map/all_to_all | solution.py:139
  76.3 5.4 %copy.346 = f32[24,64,1,1,4,128]{5,0,4,1,2,3:T(8,128)} copy(f32[24,64,1,1,4,128]{5,4,3,2,1,0:T(4,128)} %param.19) | data formatting | bytes 6291456 | tf_op jit(solution)/shard_map/reshape | solution.py:166
  83.4 3.0 %copy.253 = f32[24,64,4,1]{3,0,1,2:T(8,128)} copy(f32[24,64,4,1]{1,0,3,2:T(8,128)} %collective-permute-done.15) | data formatting | bytes 49152 | tf_op jit(solution)/shard_map/ppermute | solution.py:72
  86.4 3.0 %copy.256 = f32[24,64,4,1]{3,0,1,2:T(8,128)} copy(f32[24,64,4,1]{1,0,3,2:T(8,128)} %collective-permute-done.16) | data formatting | bytes 49152 | tf_op jit(solution)/shard_map/ppermute | solution.py:74
  89.3 4.2 %all-to-all-start.1 = ((f32[16,16,128]{2,0,1:T(8,128)}), f32[16,16,128]{2,0,1:T(8,128)}, u32[]{:S(2)}, u32[]{:S(2)}) async-start(f32[16,16,128]{2,0,1:T(8,128)} %get-tuple-element.59), calls=%async_computation.1 | async-start | bytes 262144 | tf_op jit(solution)/shard_map/all_to_all | solution.py:138
  96.0 3.2 %collective-permute-start.14 = (f32[64,4]{0,1:T(4,128)}, f32[64,4]{0,1:T(4,128)}, u32[]{:S(2)}, u32[]{:S(2)}) collective-permute-start(f32[64,4]{0,1:T(4,128)} %slice_reduce_fusion), channel_id=1, source_target_pairs={{0,1},{1,2},{2,3},{3,4},{4,5},{5,6},{6,7},{8,9},{9,10},{10,11},{11... | collective-permute-start | bytes 3080 | tf_op jit(solution)/shard_map/ppermute | solution.py:56
  105.2 4.7 %pad_maximum_fusion = (f32[24,64,4,129]{3,0,1,2:T(8,128)S(1)}, f32[24,64,4,129]{3,0,1,2:T(8,128)S(1)}) fusion(f32[24,64,4,128]{3,0,1,2:T(8,128)S(1)} %bitcast.168, f32[24,64,4,1]{3,0,1,2:T(8,128)} %copy.253, f32[24,64,4,1]{3,0,1,2:T(8,128)} %copy.256, f32[64,4,129]{2,0,1:T(8,128)S(1)} %get-tuple-element.65), kind=kLoop, calls=%fused_computation | loop fusion | flops 2377728 | bytes 9667584 | tf_op jit(solution)/shard_map/concatenate | solution.py:70
  110.8 1.9 collective-permute-start.9
  112.7 4.3 %collective-permute-start.13 = (f32[24,64,128]{2,0,1:T(8,128)}, f32[24,64,128]{2,0,1:T(8,128)}, u32[]{:S(2)}, u32[]{:S(2)}) collective-permute-start(f32[24,64,128]{2,0,1:T(8,128)} %collective-permute-done.12), channel_id=1, source_target_pairs={{8,0},{16,8},{24,16},{32,24},{40,32},{48,40},{56,48},{9,1},{17,9},... | collective-permute-start | bytes 2359304 | tf_op jit(solution)/shard_map/ppermute | solution.py:56
  117.0 2.0 collective-permute-start.11
  118.9 4.6 %copy_add_fusion = f32[24,64,4,129]{3,0,2,1:T(8,128)} fusion(f32[24,64,4,129]{3,0,1,2:T(8,128)S(1)} %get-tuple-element.53, f32[24,64,4,129]{3,0,1,2:T(8,128)S(1)} %get-tuple-element.52, f32[64,4,129]{2,1,0:T(4,128)} %copy.251), kind=kLoop, calls=%fused_computation.5 | loop fusion | flops 1585152 | bytes 9643008 | tf_op jit(solution)/shard_map/add | solution.py:182
  126.1 25.4 %collective-permute-done.11 = f32[24,64,128]{2,0,1:T(8,128)} collective-permute-done((f32[24,64,128]{2,0,1:T(8,128)}, f32[24,64,128]{2,0,1:T(8,128)}, u32[]{:S(2)}, u32[]{:S(2)}) %collective-permute-start.11) | collective-permute-done | bytes 786464 | tf_op jit(solution)/shard_map/ppermute | solution.py:56
  155.8 6.8 %fusion.7 = f32[24,64,4,128]{3,0,2,1:T(8,128)S(1)} fusion(f32[24,64,4,129]{3,0,2,1:T(8,128)} %copy_add_fusion, f32[24,64,5,128]{3,0,2,1:T(8,128)S(1)} %fusion.1, f32[64,4,128]{2,1,0:T(4,128)} %copy.242, f32[24,64,1,1,4,128]{5,4,3,2,1,0:T(4,128)S(1)} %copy-done.1), kind=kLoop, calls=%fused_computation.20 | loop fusion | flops 3932160 | bytes 19005440 | tf_op jit(solution)/shard_map/mul | solution.py:186
  164.5 8.6 %collective-permute-start.7 = (f32[3,16,16,1]{3,1,2,0:T(8,128)S(1)}, f32[3,16,16,1]{3,1,2,0:T(8,128)S(1)}, u32[]{:S(2)}, u32[]{:S(2)}) collective-permute-start(f32[3,16,16,1]{3,1,2,0:T(8,128)S(1)} %copy-done.24), channel_id=1, source_target_pairs={{0,1},{1,2},{2,3},{3,4},{4,5},{5,6},{6,7},{8,9},{9,10},{10,11},{11... | collective-permute-start | bytes 9224 | tf_op jit(solution)/shard_map/ppermute | solution.py:25
  173.1 4.7 %collective-permute-done.7 = f32[3,16,16,1]{3,1,2,0:T(8,128)S(1)} collective-permute-done((f32[3,16,16,1]{3,1,2,0:T(8,128)S(1)}, f32[3,16,16,1]{3,1,2,0:T(8,128)S(1)}, u32[]{:S(2)}, u32[]{:S(2)}) %collective-permute-start.7) | collective-permute-done | bytes 3104 | tf_op jit(solution)/shard_map/ppermute | solution.py:25
  179.6 2.1 collective-permute-done.17
  181.7 3.4 %collective-permute-start.18 = (f32[24,64,128]{2,0,1:T(8,128)}, f32[24,64,128]{2,0,1:T(8,128)}, u32[]{:S(2)}, u32[]{:S(2)}) collective-permute-start(f32[24,64,128]{2,0,1:T(8,128)} %collective-permute-done.17), channel_id=1, source_target_pairs={{0,8},{8,16},{16,24},{24,32},{32,40},{40,48},{48,56},{1,9},{9,17},... | collective-permute-start | bytes 2359304 | tf_op jit(solution)/shard_map/ppermute | solution.py:56
  185.1 3.8 %fusion.71 = (f32[24,64,4,1]{3,0,2,1:T(8,128)}, f32[24,64,4,1]{3,0,2,1:T(8,128)}) fusion(f32[24,64,4,128]{3,0,2,1:T(8,128)S(1)} %fusion.7), kind=kLoop, calls=%fused_computation.156 | loop fusion | bytes 98304 | tf_op jit(solution)/shard_map/slice | solution.py:68
  188.9 3.3 %copy.263 = f32[24,64,4,1]{1,0,3,2:T(8,128)} copy(f32[24,64,4,1]{3,0,2,1:T(8,128)} %get-tuple-element.49) | data formatting | bytes 49152 | tf_op jit(solution)/shard_map/slice | solution.py:69
  192.2 8.4 %collective-permute-start.21 = (f32[24,64,4,1]{1,0,3,2:T(8,128)}, f32[24,64,4,1]{1,0,3,2:T(8,128)}, u32[]{:S(2)}, u32[]{:S(2)}) collective-permute-start(f32[24,64,4,1]{1,0,3,2:T(8,128)} %copy.263), channel_id=1, source_target_pairs={{0,1},{1,2},{2,3},{3,4},{4,5},{5,6},{6,7},{8,9},{9,10},{10,11},{11... | collective-permute-start | bytes 73736 | tf_op jit(solution)/shard_map/ppermute | solution.py:72
  200.5 3.2 %copy.265 = f32[24,64,4,1]{1,0,3,2:T(8,128)} copy(f32[24,64,4,1]{3,0,2,1:T(8,128)} %get-tuple-element.48) | data formatting | bytes 49152 | tf_op jit(solution)/shard_map/slice | solution.py:68
  203.8 1.9 collective-permute-start.22
  205.7 4.8 %collective-permute-start.20 = (f32[24,64,128]{2,0,1:T(8,128)}, f32[24,64,128]{2,0,1:T(8,128)}, u32[]{:S(2)}, u32[]{:S(2)}) collective-permute-start(f32[24,64,128]{2,0,1:T(8,128)} %collective-permute-done.19), channel_id=1, source_target_pairs={{8,0},{16,8},{24,16},{32,24},{40,32},{48,40},{56,48},{9,1},{17,9},... | collective-permute-start | bytes 2359304 | tf_op jit(solution)/shard_map/ppermute | solution.py:56
  215.3 3.2 %copy.264 = f32[24,64,4,1]{3,0,2,1:T(8,128)} copy(f32[24,64,4,1]{1,0,3,2:T(8,128)} %collective-permute-done.21) | data formatting | bytes 49152 | tf_op jit(solution)/shard_map/ppermute | solution.py:72
  218.5 3.2 %copy.266 = f32[24,64,4,1]{3,0,2,1:T(8,128)} copy(f32[24,64,4,1]{1,0,3,2:T(8,128)} %collective-permute-done.22) | data formatting | bytes 49152 | tf_op jit(solution)/shard_map/ppermute | solution.py:74
  221.6 4.3 %fusion = f32[24,64,4,129]{3,0,2,1:T(8,128)S(1)} fusion(f32[24,64,4,128]{3,0,2,1:T(8,128)S(1)} %fusion.7, f32[24,64,4,1]{3,0,2,1:T(8,128)} %copy.264, f32[24,64,4,1]{3,0,2,1:T(8,128)} %copy.266, f32[64,4,129]{2,1,0:T(4,128)} %copy.288, f32[64,4,129]{2,1,0:T(4,128)S(1)} %copy-done.8), kind=kLoop, calls=%fused_computation.3 | loop fusion | flops 3962880 | bytes 6629376 | tf_op jit(solution)/shard_map/add | solution.py:182
  232.7 1.7 fusion.67
  235.4 4.8 %all-to-all-start.3 = ((f32[64,4,128]{2,1,0:T(4,128)}), f32[64,4,128]{2,1,0:T(4,128)S(1)}, u32[]{:S(2)}, u32[]{:S(2)}) async-start(f32[64,4,128]{2,1,0:T(4,128)} %copy.271), calls=%async_computation.3 | async-start | bytes 262144 | tf_op jit(solution)/shard_map/all_to_all | solution.py:202
  240.4 7.0 %fusion.9 = f32[24,64,1,1,4,128]{5,0,4,1,3,2:T(8,128)S(1)} fusion(f32[24,64,4,128]{3,0,2,1:T(8,128)} %copy-done.2, f32[24]{0:T(128)} %param.24, f32[64,4,128]{2,1,0:T(4,128)S(1)} %copy.275, f32[24]{0:T(128)} %param.23, f32[64,4,128]{2,1,0:T(4,128)S(1)} %bitcast.184, f32[24]{0:T(128)} %param.22, f32[64,4,128]{2,1,0:T(4,128)S(1)} %copy.274, ...), kind=kOutput, calls=%fused_computation.24 | convolution fusion | flops 233570304 | bytes 6687264 | tf_op jit(solution)/shard_map/dot_general | solution.py:210
  247.4 2.5 copy.281
  (157 shorter events, 50.2 us)
Async XLA Ops:
  0.6 239.7 %copy-start = (f32[24,24]{1,0:T(8,128)S(1)}, f32[24,24]{1,0:T(8,128)}, u32[]{:S(2)}) copy-start(f32[24,24]{1,0:T(8,128)} %param.25) | copy-start | bytes 6916
  1.5 32.5 %collective-permute-start.3 = (s32[2,16,1]{2,1,0:T(8,128)S(1)}, s32[2,16,1]{2,1,0:T(8,128)S(1)}, u32[]{:S(2)}, u32[]{:S(2)}) collective-permute-start(s32[2,16,1]{2,1,0:T(8,128)S(1)} %get-tuple-element.73), channel_id=1, source_target_pairs={{1,0},{2,1},{3,2},{4,3},{5,4},{6,5},{7,6},{9,8},{10,9},{11,10},{12... | collective-permute-start | bytes 392 | tf_op jit(solution)/shard_map/ppermute | solution.py:26
  4.1 32.1 %collective-permute-start = (s32[2,16,1]{2,1,0:T(8,128)S(1)}, s32[2,16,1]{2,1,0:T(8,128)S(1)}, u32[]{:S(2)}, u32[]{:S(2)}) collective-permute-start(s32[2,16,1]{2,1,0:T(8,128)S(1)} %get-tuple-element.72), channel_id=1, source_target_pairs={{0,1},{1,2},{2,3},{3,4},{4,5},{5,6},{6,7},{8,9},{9,10},{10,11},{11... | collective-permute-start | bytes 392 | tf_op jit(solution)/shard_map/ppermute | solution.py:25
  9.6 26.6 %collective-permute-start.2 = (s32[2,1,128]{2,1,0:T(1,128)S(1)}, s32[2,1,128]{2,1,0:T(1,128)S(1)}, u32[]{:S(2)}, u32[]{:S(2)}) collective-permute-start(s32[2,1,128]{2,1,0:T(1,128)S(1)} %get-tuple-element.71), channel_id=1, source_target_pairs={{8,0},{16,8},{24,16},{32,24},{40,32},{48,40},{56,48},{9,1},{17,9},... | collective-permute-start | bytes 3080 | tf_op jit(solution)/shard_map/ppermute | solution.py:26
  13.4 22.8 %collective-permute-start.1 = (s32[2,1,128]{2,1,0:T(1,128)S(1)}, s32[2,1,128]{2,1,0:T(1,128)S(1)}, u32[]{:S(2)}, u32[]{:S(2)}) collective-permute-start(s32[2,1,128]{2,1,0:T(1,128)S(1)} %get-tuple-element.70), channel_id=1, source_target_pairs={{0,8},{8,16},{16,24},{24,32},{32,40},{40,48},{48,56},{1,9},{9,17},... | collective-permute-start | bytes 3080 | tf_op jit(solution)/shard_map/ppermute | solution.py:25
  22.7 7.6 %copy-start.31 = (s32[16,128]{1,0:T(8,128)S(1)}, s32[16,128]{1,0:T(8,128)}, u32[]{:S(2)}) copy-start(s32[16,128]{1,0:T(8,128)} %param.18) | copy-start | bytes 24580
  22.7 7.6 %copy-start.30 = (s32[16,128]{1,0:T(8,128)S(1)}, s32[16,128]{1,0:T(8,128)}, u32[]{:S(2)}) copy-start(s32[16,128]{1,0:T(8,128)} %param.17) | copy-start | bytes 24580
  25.8 57.5 %collective-permute-start.15 = (f32[24,64,4,1]{1,0,3,2:T(8,128)}, f32[24,64,4,1]{1,0,3,2:T(8,128)}, u32[]{:S(2)}, u32[]{:S(2)}) collective-permute-start(f32[24,64,4,1]{1,0,3,2:T(8,128)} %copy.252), channel_id=1, source_target_pairs={{0,1},{1,2},{2,3},{3,4},{4,5},{5,6},{6,7},{8,9},{9,10},{10,11},{11... | collective-permute-start | bytes 73736 | tf_op jit(solution)/shard_map/ppermute | solution.py:72
  28.5 8.7 %copy-start.29 = (f32[16,16,128]{2,1,0:T(8,128)S(1)}, f32[16,16,128]{2,1,0:T(8,128)}, u32[]{:S(2)}) copy-start(f32[16,16,128]{2,1,0:T(8,128)} %param.16) | copy-start | bytes 393220
  34.0 52.4 %collective-permute-start.16 = (f32[24,64,4,1]{1,0,3,2:T(8,128)}, f32[24,64,4,1]{1,0,3,2:T(8,128)}, u32[]{:S(2)}, u32[]{:S(2)}) collective-permute-start(f32[24,64,4,1]{1,0,3,2:T(8,128)} %copy.255), channel_id=1, source_target_pairs={{1,0},{2,1},{3,2},{4,3},{5,4},{6,5},{7,6},{9,8},{10,9},{11,10},{12... | collective-permute-start | bytes 73736 | tf_op jit(solution)/shard_map/ppermute | solution.py:74
  39.5 7.5 %all-to-all-start = ((f32[4,1,16,128]{3,2,1,0:T(8,128)}), f32[4,1,16,128]{3,2,1,0:T(8,128)S(1)}, u32[]{:S(2)}, u32[]{:S(2)}) async-start(f32[4,1,16,128]{3,2,1,0:T(8,128)} %broadcast_in_dim.10), calls=%async_computation | async-start | bytes 65536 | tf_op jit(solution)/shard_map/all_to_all | solution.py:39
  47.0 11.9 %copy-start.5 = (f32[16,18,130]{2,0,1:T(8,128)S(1)}, f32[16,18,130]{2,0,1:T(8,128)}, u32[]{:S(2)}) copy-start(f32[16,18,130]{2,0,1:T(8,128)} %copy-done.4) | copy-start | bytes 449284
  47.1 20.7 %copy-start.12 = (f32[16,16,129]{2,0,1:T(8,128)S(1)}, f32[16,16,129]{2,0,1:T(8,128)}, u32[]{:S(2)}) copy-start(f32[16,16,129]{2,0,1:T(8,128)} %slice_multiply_fusion) | copy-start | bytes 396292
  50.0 15.1 %collective-permute-start.6 = (f32[3,16,16,1]{3,1,2,0:T(8,128)S(1)}, f32[3,16,16,1]{3,1,2,0:T(8,128)S(1)}, u32[]{:S(2)}, u32[]{:S(2)}) collective-permute-start(f32[3,16,16,1]{3,1,2,0:T(8,128)S(1)} %get-tuple-element.57), channel_id=1, source_target_pairs={{1,0},{2,1},{3,2},{4,3},{5,4},{6,5},{7,6},{9,8},{10,9},{11,10},{12... | collective-permute-start | bytes 9224 | tf_op jit(solution)/shard_map/ppermute | solution.py:26
  52.7 14.0 %collective-permute-start.4 = (f32[3,16,1,128]{3,1,2,0:T(8,128)S(1)}, f32[3,16,1,128]{3,1,2,0:T(8,128)S(1)}, u32[]{:S(2)}, u32[]{:S(2)}) collective-permute-start(f32[3,16,1,128]{3,1,2,0:T(8,128)S(1)} %get-tuple-element.61), channel_id=1, source_target_pairs={{8,0},{16,8},{24,16},{32,24},{40,32},{48,40},{56,48},{9,1},{17,9},... | collective-permute-start | bytes 73736 | tf_op jit(solution)/shard_map/ppermute | solution.py:26
  57.0 9.7 %collective-permute-start.5 = (f32[3,16,1,128]{3,1,2,0:T(8,128)S(1)}, f32[3,16,1,128]{3,1,2,0:T(8,128)S(1)}, u32[]{:S(2)}, u32[]{:S(2)}) collective-permute-start(f32[3,16,1,128]{3,1,2,0:T(8,128)S(1)} %get-tuple-element.60), channel_id=1, source_target_pairs={{0,8},{8,16},{16,24},{24,32},{32,40},{40,48},{48,56},{1,9},{9,17},... | collective-permute-start | bytes 73736 | tf_op jit(solution)/shard_map/ppermute | solution.py:25
  59.1 10.5 %copy-start.18 = (f32[16,17,128]{2,0,1:T(8,128)}, f32[16,17,128]{2,0,1:T(8,128)S(1)}, u32[]{:S(2)}) copy-start(f32[16,17,128]{2,0,1:T(8,128)S(1)} %slice_multiply_fusion.1) | copy-start | bytes 417796
  65.1 47.6 %collective-permute-start.12 = (f32[24,64,128]{2,0,1:T(8,128)}, f32[24,64,128]{2,0,1:T(8,128)}, u32[]{:S(2)}, u32[]{:S(2)}) collective-permute-start(f32[24,64,128]{2,0,1:T(8,128)} %get-tuple-element.51), channel_id=1, source_target_pairs={{0,192},{64,0},{128,64},{192,128},{1,193},{65,1},{129,65},{193,129... | collective-permute-start | bytes 2359304 | tf_op jit(solution)/shard_map/ppermute | solution.py:61
  66.7 50.2 %collective-permute-start.10 = (f32[24,64,128]{2,0,1:T(8,128)}, f32[24,64,128]{2,0,1:T(8,128)}, u32[]{:S(2)}, u32[]{:S(2)}) collective-permute-start(f32[24,64,128]{2,0,1:T(8,128)} %get-tuple-element.50), channel_id=1, source_target_pairs={{0,64},{64,128},{128,192},{192,0},{1,65},{65,129},{129,193},{193,1... | collective-permute-start | bytes 2359304 | tf_op jit(solution)/shard_map/ppermute | solution.py:61
  69.6 19.7 %all-to-all-start.2 = ((f32[16,16,128]{2,0,1:T(8,128)}), f32[16,16,128]{2,0,1:T(8,128)}, u32[]{:S(2)}, u32[]{:S(2)}) async-start(f32[16,16,128]{2,0,1:T(8,128)} %get-tuple-element.58), calls=%async_computation.2 | async-start | bytes 262144 | tf_op jit(solution)/shard_map/all_to_all | solution.py:139
  89.3 9.9 %all-to-all-start.1 = ((f32[16,16,128]{2,0,1:T(8,128)}), f32[16,16,128]{2,0,1:T(8,128)}, u32[]{:S(2)}, u32[]{:S(2)}) async-start(f32[16,16,128]{2,0,1:T(8,128)} %get-tuple-element.59), calls=%async_computation.1 | async-start | bytes 262144 | tf_op jit(solution)/shard_map/all_to_all | solution.py:138
  96.0 6.6 %collective-permute-start.14 = (f32[64,4]{0,1:T(4,128)}, f32[64,4]{0,1:T(4,128)}, u32[]{:S(2)}, u32[]{:S(2)}) collective-permute-start(f32[64,4]{0,1:T(4,128)} %slice_reduce_fusion), channel_id=1, source_target_pairs={{0,1},{1,2},{2,3},{3,4},{4,5},{5,6},{6,7},{8,9},{9,10},{10,11},{11... | collective-permute-start | bytes 3080 | tf_op jit(solution)/shard_map/ppermute | solution.py:56
  101.4 9.3 %collective-permute-start.8 = (f32[64,128]{1,0:T(8,128)}, f32[64,128]{1,0:T(8,128)}, u32[]{:S(2)}, u32[]{:S(2)}) collective-permute-start(f32[64,128]{1,0:T(8,128)} %slice_bitcast_fusion.7), channel_id=1, source_target_pairs={{0,64},{64,128},{128,192},{192,0},{1,65},{65,129},{129,193},{193,1... | collective-permute-start | bytes 98312 | tf_op jit(solution)/shard_map/ppermute | solution.py:61
  105.2 4.7 %copy-start.9 = (f32[64,4,129]{2,0,1:T(8,128)}, f32[64,4,129]{2,0,1:T(8,128)S(1)}, u32[]{:S(2)}) copy-start(f32[64,4,129]{2,0,1:T(8,128)S(1)} %get-tuple-element.65) | copy-start | bytes 396292
  110.8 12.8 %collective-permute-start.9 = (f32[64,128]{1,0:T(8,128)}, f32[64,128]{1,0:T(8,128)S(1)}, u32[]{:S(2)}, u32[]{:S(2)}) collective-permute-start(f32[64,128]{1,0:T(8,128)} %collective-permute-done.8), channel_id=1, source_target_pairs={{0,8},{8,16},{16,24},{24,32},{32,40},{40,48},{48,56},{1,9},{9,17},... | collective-permute-start | bytes 98312 | tf_op jit(solution)/shard_map/ppermute | solution.py:56
  112.7 40.0 %collective-permute-start.13 = (f32[24,64,128]{2,0,1:T(8,128)}, f32[24,64,128]{2,0,1:T(8,128)}, u32[]{:S(2)}, u32[]{:S(2)}) collective-permute-start(f32[24,64,128]{2,0,1:T(8,128)} %collective-permute-done.12), channel_id=1, source_target_pairs={{8,0},{16,8},{24,16},{32,24},{40,32},{48,40},{56,48},{9,1},{17,9},... | collective-permute-start | bytes 2359304 | tf_op jit(solution)/shard_map/ppermute | solution.py:56
  117.0 34.5 %collective-permute-start.11 = (f32[24,64,128]{2,0,1:T(8,128)}, f32[24,64,128]{2,0,1:T(8,128)}, u32[]{:S(2)}, u32[]{:S(2)}) collective-permute-start(f32[24,64,128]{2,0,1:T(8,128)} %collective-permute-done.10), channel_id=1, source_target_pairs={{0,8},{8,16},{16,24},{24,32},{32,40},{40,48},{48,56},{1,9},{9,17},... | collective-permute-start | bytes 2359304 | tf_op jit(solution)/shard_map/ppermute | solution.py:56
  123.5 30.4 %copy-start.3 = (f32[24,64,1,1,4,128]{5,0,4,1,2,3:T(8,128)S(1)}, f32[24,64,1,1,4,128]{5,0,4,1,2,3:T(8,128)}, u32[]{:S(2)}) copy-start(f32[24,64,1,1,4,128]{5,0,4,1,2,3:T(8,128)} %copy.346) | copy-start | bytes 9437188
  125.4 28.5 %copy-start.16 = (f32[64,5,128]{2,0,1:T(8,128)}, f32[64,5,128]{2,0,1:T(8,128)S(1)}, u32[]{:S(2)}) copy-start(f32[64,5,128]{2,0,1:T(8,128)S(1)} %get-tuple-element.67) | copy-start | bytes 491524
  162.6 15.3 %copy-start.7 = (f32[3,16,18,129]{3,1,2,0:T(8,128)S(1)}, f32[3,16,18,129]{3,1,2,0:T(8,128)}, u32[]{:S(2)}) copy-start(f32[3,16,18,129]{3,1,2,0:T(8,128)} %copy-done.6) | copy-start | bytes 1337476
  162.6 15.3 %copy-start.13 = (f32[16,16,129]{2,0,1:T(8,128)S(1)}, f32[16,16,129]{2,0,1:T(8,128)}, u32[]{:S(2)}) copy-start(f32[16,16,129]{2,0,1:T(8,128)} %slice_multiply_fusion) | copy-start | bytes 396292
  162.6 15.3 %copy-start.26 = (f32[3,16,1,128]{3,1,2,0:T(8,128)S(1)}, f32[3,16,1,128]{3,1,2,0:T(8,128)}, u32[]{:S(2)}) copy-start(f32[3,16,1,128]{3,1,2,0:T(8,128)} %copy-done.25) | copy-start | bytes 73732
  162.6 15.2 %copy-start.28 = (f32[3,16,1,128]{3,1,2,0:T(8,128)S(1)}, f32[3,16,1,128]{3,1,2,0:T(8,128)}, u32[]{:S(2)}) copy-start(f32[3,16,1,128]{3,1,2,0:T(8,128)} %copy-done.27) | copy-start | bytes 73732
  162.6 16.1 %copy-start.19 = (f32[16,17,128]{2,0,1:T(8,128)S(1)}, f32[16,17,128]{2,0,1:T(8,128)}, u32[]{:S(2)}) copy-start(f32[16,17,128]{2,0,1:T(8,128)} %copy-done.18) | copy-start | bytes 417796
  163.6 18.1 %collective-permute-start.17 = (f32[24,64,128]{2,0,1:T(8,128)S(1)}, f32[24,64,128]{2,0,1:T(8,128)}, u32[]{:S(2)}, u32[]{:S(2)}) collective-permute-start(f32[24,64,128]{2,0,1:T(8,128)S(1)} %get-tuple-element.47), channel_id=1, source_target_pairs={{0,64},{64,128},{128,192},{192,0},{1,65},{65,129},{129,193},{193,1... | collective-permute-start | bytes 2359304 | tf_op jit(solution)/shard_map/ppermute | solution.py:61
  164.5 13.3 %collective-permute-start.7 = (f32[3,16,16,1]{3,1,2,0:T(8,128)S(1)}, f32[3,16,16,1]{3,1,2,0:T(8,128)S(1)}, u32[]{:S(2)}, u32[]{:S(2)}) collective-permute-start(f32[3,16,16,1]{3,1,2,0:T(8,128)S(1)} %copy-done.24), channel_id=1, source_target_pairs={{0,1},{1,2},{2,3},{3,4},{4,5},{5,6},{6,7},{8,9},{9,10},{10,11},{11... | collective-permute-start | bytes 9224 | tf_op jit(solution)/shard_map/ppermute | solution.py:25
  178.1 27.6 %collective-permute-start.19 = (f32[24,64,128]{2,0,1:T(8,128)}, f32[24,64,128]{2,0,1:T(8,128)}, u32[]{:S(2)}, u32[]{:S(2)}) collective-permute-start(f32[24,64,128]{2,0,1:T(8,128)} %get-tuple-element.46), channel_id=1, source_target_pairs={{0,192},{64,0},{128,64},{192,128},{1,193},{65,1},{129,65},{193,129... | collective-permute-start | bytes 2359304 | tf_op jit(solution)/shard_map/ppermute | solution.py:61
  181.7 44.3 %collective-permute-start.18 = (f32[24,64,128]{2,0,1:T(8,128)}, f32[24,64,128]{2,0,1:T(8,128)}, u32[]{:S(2)}, u32[]{:S(2)}) collective-permute-start(f32[24,64,128]{2,0,1:T(8,128)} %collective-permute-done.17), channel_id=1, source_target_pairs={{0,8},{8,16},{16,24},{24,32},{32,40},{40,48},{48,56},{1,9},{9,17},... | collective-permute-start | bytes 2359304 | tf_op jit(solution)/shard_map/ppermute | solution.py:56
  188.9 24.1 %copy-start.21 = (f32[16,16,128]{2,0,1:T(8,128)S(1)}, f32[16,16,128]{2,0,1:T(8,128)}, u32[]{:S(2)}) copy-start(f32[16,16,128]{2,0,1:T(8,128)} %get-tuple-element.58) | copy-start | bytes 393220
  188.9 25.5 %copy-start.10 = (f32[64,4,129]{2,0,1:T(8,128)S(1)}, f32[64,4,129]{2,0,1:T(8,128)}, u32[]{:S(2)}) copy-start(f32[64,4,129]{2,0,1:T(8,128)} %copy-done.9) | copy-start | bytes 396292
  192.2 23.1 %collective-permute-start.21 = (f32[24,64,4,1]{1,0,3,2:T(8,128)}, f32[24,64,4,1]{1,0,3,2:T(8,128)}, u32[]{:S(2)}, u32[]{:S(2)}) collective-permute-start(f32[24,64,4,1]{1,0,3,2:T(8,128)} %copy.263), channel_id=1, source_target_pairs={{0,1},{1,2},{2,3},{3,4},{4,5},{5,6},{6,7},{8,9},{9,10},{10,11},{11... | collective-permute-start | bytes 73736 | tf_op jit(solution)/shard_map/ppermute | solution.py:72
  203.8 14.7 %collective-permute-start.22 = (f32[24,64,4,1]{1,0,3,2:T(8,128)}, f32[24,64,4,1]{1,0,3,2:T(8,128)}, u32[]{:S(2)}, u32[]{:S(2)}) collective-permute-start(f32[24,64,4,1]{1,0,3,2:T(8,128)} %copy.265), channel_id=1, source_target_pairs={{1,0},{2,1},{3,2},{4,3},{5,4},{6,5},{7,6},{9,8},{10,9},{11,10},{12... | collective-permute-start | bytes 73736 | tf_op jit(solution)/shard_map/ppermute | solution.py:74
  205.7 21.6 %collective-permute-start.20 = (f32[24,64,128]{2,0,1:T(8,128)}, f32[24,64,128]{2,0,1:T(8,128)}, u32[]{:S(2)}, u32[]{:S(2)}) collective-permute-start(f32[24,64,128]{2,0,1:T(8,128)} %collective-permute-done.19), channel_id=1, source_target_pairs={{8,0},{16,8},{24,16},{32,24},{40,32},{48,40},{56,48},{9,1},{17,9},... | collective-permute-start | bytes 2359304 | tf_op jit(solution)/shard_map/ppermute | solution.py:56
  215.3 6.4 %copy-start.8 = (f32[64,4,129]{2,1,0:T(4,128)S(1)}, f32[64,4,129]{2,1,0:T(4,128)}, u32[]{:S(2)}) copy-start(f32[64,4,129]{2,1,0:T(4,128)} %copy.251) | copy-start | bytes 396292
  229.6 3.1 %copy-start.33 = (f32[24]{0:T(128)S(1)}, f32[24]{0:T(128)}, u32[]{:S(2)}) copy-start(f32[24]{0:T(128)} %param.21) | copy-start | bytes 292
  231.0 3.4 %copy-start.32 = (pred[4,128]{1,0:T(4,128)(4,1)S(1)}, pred[4,128]{1,0:T(4,128)(4,1)}, u32[]{:S(2)}) copy-start(pred[4,128]{1,0:T(4,128)(4,1)} %dynamic-slice_compare_fusion) | copy-start | bytes 1540
  231.0 3.4 %copy-start.34 = (f32[1,1,4,128]{3,2,1,0:T(4,128)S(1)}, f32[1,1,4,128]{3,2,1,0:T(4,128)}, u32[]{:S(2)}) copy-start(f32[1,1,4,128]{3,2,1,0:T(4,128)} %param.20) | copy-start | bytes 6148
  235.4 14.5 %all-to-all-start.3 = ((f32[64,4,128]{2,1,0:T(4,128)}), f32[64,4,128]{2,1,0:T(4,128)S(1)}, u32[]{:S(2)}, u32[]{:S(2)}) async-start(f32[64,4,128]{2,1,0:T(4,128)} %copy.271), calls=%async_computation.3 | async-start | bytes 262144 | tf_op jit(solution)/shard_map/all_to_all | solution.py:202
  (14 other events, 23.6 us)
where the time goes:
time: 254 us; the launch traced here: 252 us
  starting transfers between devices  88.2 us (35%)
  local copies, waits for them, and re-layouts  66.7 us (26%)
  other arithmetic  46.3 us (18%)
  waiting for transfers between devices  39.6 us (16%)
  matrix products  10.1 us (4%)
    ppermute x6, waiting for transfers between devices, from_behind(): return lax.ppermute(x, axis, pairs)  25.4 us
    ppermute x6, starting transfers between devices, from_behind(): return lax.ppermute(x, axis, pairs)  19.5 us
    unnamed x79, local copies, waits for them, and re-layouts  17.6 us
    ppermute x4, starting transfers between devices, padded(): lax.ppermute(last, axis, up)  17.2 us
    ppermute x4, starting transfers between devices, padded(): lax.ppermute(first, axis, [(b, a) for a, b in up])  13.3 us
    ppermute x2, starting transfers between devices, extended_2(): lax.ppermute(tail, axis, [(i, (i + 1) % count) for i in range(ends)])  11 us
    slice x3, local copies, waits for them, and re-layouts, extended_2(): head = lax.slice_in_dim(cells, 0, width, axis=dim)  10.1 us
    slice x3, local copies, waits for them, and re-layouts, extended_2(): lax.slice_in_dim(cells, cells.shape[dim] - width, cells.shape[dim], axis=...  10 us
  transfers between devices with their start and end apart: 27, of which 5 were waited for; matrix products, arithmetic and copies ran while one was open for 39% of the time, Pallas kernels for 0%

commit v1 on v0

--- a/solution.py
+++ b/solution.py
@@ -136,7 +136,12 @@
     )
     east_column, north_column = (
         lax.all_to_all(east_new, "comp", split_axis=1, concat_axis=0, tiled=True),
-        lax.all_to_all(north_new, "comp", split_axis=1, concat_axis=0, tiled=True),
+        jnp.concatenate(
+            lax.all_to_all(
+                jnp.stack(jnp.split(north_new, lax.axis_size("comp"), axis=1)), "comp", 0, 0
+            ),
+            axis=0,
+        ),
     )
     scalar_pair = padded_field[:2]
     flux_east = face_east[None] * (scalar_pair[:, :, 1:, 1:-1] - scalar_pair[:, :, :-1, 1:-1])

time: 254 us -> 256 us (level)
    unnamed x79 -> x81, local copies, waits for them, and re-layouts: 17.6 us -> 18.3 us
where the time goes in v1:
time: 256 us; the launch traced here: 254 us
  starting transfers between devices  88.1 us (34%)
  local copies, waits for them, and re-layouts  67.4 us (26%)
  other arithmetic  46.9 us (18%)
  waiting for transfers between devices  39.7 us (16%)
  matrix products  10.1 us (4%)
    ppermute x6, waiting for transfers between devices, from_behind(): return lax.ppermute(x, axis, pairs)  25.5 us
    ppermute x6, starting transfers between devices, from_behind(): return lax.ppermute(x, axis, pairs)  19.5 us
    unnamed x81, local copies, waits for them, and re-layouts  18.3 us
    ppermute x4, starting transfers between devices, padded(): lax.ppermute(last, axis, up)  17.2 us
    ppermute x4, starting transfers between devices, padded(): lax.ppermute(first, axis, [(b, a) for a, b in up])  13.3 us
    ppermute x2, starting transfers between devices, extended_2(): lax.ppermute(tail, axis, [(i, (i + 1) % count) for i in range(ends)])  11 us
    slice x3, local copies, waits for them, and re-layouts, extended_2(): head = lax.slice_in_dim(cells, 0, width, axis=dim)  10.1 us
    slice x3, local copies, waits for them, and re-layouts, extended_2(): lax.slice_in_dim(cells, cells.shape[dim] - width, cells.shape[dim], axis=...  10.1 us
  transfers between devices with their start and end apart: 27, of which 5 were waited for; matrix products, arithmetic and copies ran while one was open for 39% of the time, Pallas kernels for 0%

profile of v1, /device:TPU:15, one launch (start us, length us, event | category | flops | bytes accessed | tf_op | source)
XLA Modules:
  0.0 253.7 jit_solution(1476905875196535893)
XLA Ops:
  1.5 2.6 %collective-permute-start.3 = (s32[2,16,1]{2,1,0:T(8,128)S(1)}, s32[2,16,1]{2,1,0:T(8,128)S(1)}, u32[]{:S(2)}, u32[]{:S(2)}) collective-permute-start(s32[2,16,1]{2,1,0:T(8,128)S(1)} %get-tuple-element.77), channel_id=1, source_target_pairs={{1,0},{2,1},{3,2},{4,3},{5,4},{6,5},{7,6},{9,8},{10,9},{11,10},{12... | collective-permute-start | bytes 392 | tf_op jit(solution)/shard_map/ppermute | solution.py:26
  4.1 4.8 %collective-permute-start = (s32[2,16,1]{2,1,0:T(8,128)S(1)}, s32[2,16,1]{2,1,0:T(8,128)S(1)}, u32[]{:S(2)}, u32[]{:S(2)}) collective-permute-start(s32[2,16,1]{2,1,0:T(8,128)S(1)} %get-tuple-element.76), channel_id=1, source_target_pairs={{0,1},{1,2},{2,3},{3,4},{4,5},{5,6},{6,7},{8,9},{9,10},{10,11},{11... | collective-permute-start | bytes 392 | tf_op jit(solution)/shard_map/ppermute | solution.py:25
  9.6 3.8 %collective-permute-start.2 = (s32[2,1,128]{2,1,0:T(1,128)S(1)}, s32[2,1,128]{2,1,0:T(1,128)S(1)}, u32[]{:S(2)}, u32[]{:S(2)}) collective-permute-start(s32[2,1,128]{2,1,0:T(1,128)S(1)} %get-tuple-element.75), channel_id=1, source_target_pairs={{8,0},{16,8},{24,16},{32,24},{40,32},{48,40},{56,48},{9,1},{17,9},... | collective-permute-start | bytes 3080 | tf_op jit(solution)/shard_map/ppermute | solution.py:26
  13.4 1.9 collective-permute-start.1
  15.4 3.7 %copy.347 = f32[24,64,1,1,4,128]{5,0,1,4,3,2:T(8,128)S(1)} copy(f32[24,64,1,1,4,128]{5,4,3,2,1,0:T(4,128)} %param.19) | data formatting | bytes 6291456 | tf_op args[6]
  19.1 3.7 %fusion.72 = (f32[24,64,4,1]{3,0,1,2:T(8,128)}, f32[24,64,4,1]{3,0,1,2:T(8,128)}) fusion(f32[24,64,4,128]{3,0,1,2:T(8,128)S(1)} %bitcast.171), kind=kLoop, calls=%fused_computation.162 | loop fusion | bytes 98304 | tf_op jit(solution)/shard_map/slice | solution.py:69
  22.7 3.1 %copy.252 = f32[24,64,4,1]{1,0,3,2:T(8,128)} copy(f32[24,64,4,1]{3,0,1,2:T(8,128)} %get-tuple-element.54) | data formatting | bytes 49152 | tf_op jit(solution)/shard_map/slice | solution.py:69
  25.9 2.7 %collective-permute-start.15 = (f32[24,64,4,1]{1,0,3,2:T(8,128)}, f32[24,64,4,1]{1,0,3,2:T(8,128)}, u32[]{:S(2)}, u32[]{:S(2)}) collective-permute-start(f32[24,64,4,1]{1,0,3,2:T(8,128)} %copy.252), channel_id=1, source_target_pairs={{0,1},{1,2},{2,3},{3,4},{4,5},{5,6},{6,7},{8,9},{9,10},{10,11},{11... | collective-permute-start | bytes 73736 | tf_op jit(solution)/shard_map/ppermute | solution.py:72
  30.9 3.1 %copy.255 = f32[24,64,4,1]{1,0,3,2:T(8,128)} copy(f32[24,64,4,1]{3,0,1,2:T(8,128)} %get-tuple-element.55) | data formatting | bytes 49152 | tf_op jit(solution)/shard_map/slice | solution.py:68
  34.0 2.2 collective-permute-start.16
  37.2 1.7 fusion.70
  39.5 4.3 %all-to-all-start = ((f32[4,1,16,128]{3,2,1,0:T(8,128)}), f32[4,1,16,128]{3,2,1,0:T(8,128)S(1)}, u32[]{:S(2)}, u32[]{:S(2)}) async-start(f32[4,1,16,128]{3,2,1,0:T(8,128)} %broadcast_in_dim.10), calls=%async_computation | async-start | bytes 65536 | tf_op jit(solution)/shard_map/all_to_all | solution.py:39
  43.9 1.9 slice_multiply_fusion
  50.0 2.7 %collective-permute-start.6 = (f32[3,16,16,1]{3,1,2,0:T(8,128)S(1)}, f32[3,16,16,1]{3,1,2,0:T(8,128)S(1)}, u32[]{:S(2)}, u32[]{:S(2)}) collective-permute-start(f32[3,16,16,1]{3,1,2,0:T(8,128)S(1)} %get-tuple-element.57), channel_id=1, source_target_pairs={{1,0},{2,1},{3,2},{4,3},{5,4},{6,5},{7,6},{9,8},{10,9},{11,10},{12... | collective-permute-start | bytes 9224 | tf_op jit(solution)/shard_map/ppermute | solution.py:26
  52.7 4.3 %collective-permute-start.4 = (f32[3,16,1,128]{3,1,2,0:T(8,128)S(1)}, f32[3,16,1,128]{3,1,2,0:T(8,128)S(1)}, u32[]{:S(2)}, u32[]{:S(2)}) collective-permute-start(f32[3,16,1,128]{3,1,2,0:T(8,128)S(1)} %get-tuple-element.61), channel_id=1, source_target_pairs={{8,0},{16,8},{24,16},{32,24},{40,32},{48,40},{56,48},{9,1},{17,9},... | collective-permute-start | bytes 73736 | tf_op jit(solution)/shard_map/ppermute | solution.py:26
  57.0 1.9 collective-permute-start.5
  59.1 6.0 %collective-permute-done.6 = f32[3,16,16,1]{3,1,2,0:T(8,128)S(1)} collective-permute-done((f32[3,16,16,1]{3,1,2,0:T(8,128)S(1)}, f32[3,16,16,1]{3,1,2,0:T(8,128)S(1)}, u32[]{:S(2)}, u32[]{:S(2)}) %collective-permute-start.6) | collective-permute-done | bytes 3104 | tf_op jit(solution)/shard_map/ppermute | solution.py:26
  67.8 1.8 fusion.48
  70.9 5.4 %all-to-all-start.2 = ((f32[4,16,4,128]{3,1,2,0:T(8,128)}), f32[4,16,4,128]{3,1,2,0:T(8,128)}, u32[]{:S(2)}, u32[]{:S(2)}) async-start(f32[4,16,4,128]{3,1,2,0:T(8,128)} %pad_maximum_fusion.14), calls=%async_computation.2 | async-start | bytes 262144 | tf_op jit(solution)/shard_map/all_to_all | solution.py:140
  77.6 5.4 %copy.346 = f32[24,64,1,1,4,128]{5,0,4,1,2,3:T(8,128)} copy(f32[24,64,1,1,4,128]{5,4,3,2,1,0:T(4,128)} %param.19) | data formatting | bytes 6291456 | tf_op jit(solution)/shard_map/reshape | solution.py:171
  84.6 3.0 %copy.253 = f32[24,64,4,1]{3,0,1,2:T(8,128)} copy(f32[24,64,4,1]{1,0,3,2:T(8,128)} %collective-permute-done.15) | data formatting | bytes 49152 | tf_op jit(solution)/shard_map/ppermute | solution.py:72
  87.6 3.0 %copy.256 = f32[24,64,4,1]{3,0,1,2:T(8,128)} copy(f32[24,64,4,1]{1,0,3,2:T(8,128)} %collective-permute-done.16) | data formatting | bytes 49152 | tf_op jit(solution)/shard_map/ppermute | solution.py:74
  90.6 4.2 %all-to-all-start.1 = ((f32[16,16,128]{2,0,1:T(8,128)}), f32[16,16,128]{2,0,1:T(8,128)}, u32[]{:S(2)}, u32[]{:S(2)}) async-start(f32[16,16,128]{2,0,1:T(8,128)} %get-tuple-element.59), calls=%async_computation.1 | async-start | bytes 262144 | tf_op jit(solution)/shard_map/all_to_all | solution.py:138
  97.2 3.2 %collective-permute-start.14 = (f32[64,4]{0,1:T(4,128)}, f32[64,4]{0,1:T(4,128)}, u32[]{:S(2)}, u32[]{:S(2)}) collective-permute-start(f32[64,4]{0,1:T(4,128)} %slice_reduce_fusion), channel_id=1, source_target_pairs={{0,1},{1,2},{2,3},{3,4},{4,5},{5,6},{6,7},{8,9},{9,10},{10,11},{11... | collective-permute-start | bytes 3080 | tf_op jit(solution)/shard_map/ppermute | solution.py:56
  106.4 4.7 %pad_maximum_fusion = (f32[24,64,4,129]{3,0,1,2:T(8,128)S(1)}, f32[24,64,4,129]{3,0,1,2:T(8,128)S(1)}) fusion(f32[24,64,4,128]{3,0,1,2:T(8,128)S(1)} %bitcast.173, f32[24,64,4,1]{3,0,1,2:T(8,128)} %copy.253, f32[24,64,4,1]{3,0,1,2:T(8,128)} %copy.256, f32[64,4,129]{2,0,1:T(8,128)S(1)} %get-tuple-element.65), kind=kLoop, calls=%fused_computation | loop fusion | flops 2377728 | bytes 9667584 | tf_op jit(solution)/shard_map/concatenate | solution.py:70
  112.0 1.9 collective-permute-start.9
  113.9 4.3 %collective-permute-start.13 = (f32[24,64,128]{2,0,1:T(8,128)}, f32[24,64,128]{2,0,1:T(8,128)}, u32[]{:S(2)}, u32[]{:S(2)}) collective-permute-start(f32[24,64,128]{2,0,1:T(8,128)} %collective-permute-done.12), channel_id=1, source_target_pairs={{8,0},{16,8},{24,16},{32,24},{40,32},{48,40},{56,48},{9,1},{17,9},... | collective-permute-start | bytes 2359304 | tf_op jit(solution)/shard_map/ppermute | solution.py:56
  118.2 1.9 collective-permute-start.11
  120.2 4.6 %copy_add_fusion = f32[24,64,4,129]{3,0,2,1:T(8,128)} fusion(f32[24,64,4,129]{3,0,1,2:T(8,128)S(1)} %get-tuple-element.53, f32[24,64,4,129]{3,0,1,2:T(8,128)S(1)} %get-tuple-element.52, f32[64,4,129]{2,1,0:T(4,128)} %copy.251), kind=kLoop, calls=%fused_computation.5 | loop fusion | flops 1585152 | bytes 9643008 | tf_op jit(solution)/shard_map/add | solution.py:187
  127.3 25.5 %collective-permute-done.11 = f32[24,64,128]{2,0,1:T(8,128)} collective-permute-done((f32[24,64,128]{2,0,1:T(8,128)}, f32[24,64,128]{2,0,1:T(8,128)}, u32[]{:S(2)}, u32[]{:S(2)}) %collective-permute-start.11) | collective-permute-done | bytes 786464 | tf_op jit(solution)/shard_map/ppermute | solution.py:56
  157.1 6.8 %fusion.7 = f32[24,64,4,128]{3,0,2,1:T(8,128)S(1)} fusion(f32[24,64,4,129]{3,0,2,1:T(8,128)} %copy_add_fusion, f32[24,64,5,128]{3,0,2,1:T(8,128)S(1)} %fusion.1, f32[64,4,128]{2,1,0:T(4,128)} %copy.242, f32[24,64,1,1,4,128]{5,4,3,2,1,0:T(4,128)S(1)} %copy-done.1), kind=kLoop, calls=%fused_computation.20 | loop fusion | flops 3932160 | bytes 19005440 | tf_op jit(solution)/shard_map/mul | solution.py:191
  165.8 8.5 %collective-permute-start.7 = (f32[3,16,16,1]{3,1,2,0:T(8,128)S(1)}, f32[3,16,16,1]{3,1,2,0:T(8,128)S(1)}, u32[]{:S(2)}, u32[]{:S(2)}) collective-permute-start(f32[3,16,16,1]{3,1,2,0:T(8,128)S(1)} %copy-done.25), channel_id=1, source_target_pairs={{0,1},{1,2},{2,3},{3,4},{4,5},{5,6},{6,7},{8,9},{9,10},{10,11},{11... | collective-permute-start | bytes 9224 | tf_op jit(solution)/shard_map/ppermute | solution.py:25
  174.4 4.7 %collective-permute-done.7 = f32[3,16,16,1]{3,1,2,0:T(8,128)S(1)} collective-permute-done((f32[3,16,16,1]{3,1,2,0:T(8,128)S(1)}, f32[3,16,16,1]{3,1,2,0:T(8,128)S(1)}, u32[]{:S(2)}, u32[]{:S(2)}) %collective-permute-start.7) | collective-permute-done | bytes 3104 | tf_op jit(solution)/shard_map/ppermute | solution.py:25
  180.9 2.1 collective-permute-done.17
  183.0 3.4 %collective-permute-start.18 = (f32[24,64,128]{2,0,1:T(8,128)}, f32[24,64,128]{2,0,1:T(8,128)}, u32[]{:S(2)}, u32[]{:S(2)}) collective-permute-start(f32[24,64,128]{2,0,1:T(8,128)} %collective-permute-done.17), channel_id=1, source_target_pairs={{0,8},{8,16},{16,24},{24,32},{32,40},{40,48},{48,56},{1,9},{9,17},... | collective-permute-start | bytes 2359304 | tf_op jit(solution)/shard_map/ppermute | solution.py:56
  186.4 3.8 %fusion.71 = (f32[24,64,4,1]{3,0,2,1:T(8,128)}, f32[24,64,4,1]{3,0,2,1:T(8,128)}) fusion(f32[24,64,4,128]{3,0,2,1:T(8,128)S(1)} %fusion.7), kind=kLoop, calls=%fused_computation.161 | loop fusion | bytes 98304 | tf_op jit(solution)/shard_map/slice | solution.py:68
  190.2 3.3 %copy.263 = f32[24,64,4,1]{1,0,3,2:T(8,128)} copy(f32[24,64,4,1]{3,0,2,1:T(8,128)} %get-tuple-element.49) | data formatting | bytes 49152 | tf_op jit(solution)/shard_map/slice | solution.py:69
  193.5 8.3 %collective-permute-start.21 = (f32[24,64,4,1]{1,0,3,2:T(8,128)}, f32[24,64,4,1]{1,0,3,2:T(8,128)}, u32[]{:S(2)}, u32[]{:S(2)}) collective-permute-start(f32[24,64,4,1]{1,0,3,2:T(8,128)} %copy.263), channel_id=1, source_target_pairs={{0,1},{1,2},{2,3},{3,4},{4,5},{5,6},{6,7},{8,9},{9,10},{10,11},{11... | collective-permute-start | bytes 73736 | tf_op jit(solution)/shard_map/ppermute | solution.py:72
  201.8 3.2 %copy.265 = f32[24,64,4,1]{1,0,3,2:T(8,128)} copy(f32[24,64,4,1]{3,0,2,1:T(8,128)} %get-tuple-element.48) | data formatting | bytes 49152 | tf_op jit(solution)/shard_map/slice | solution.py:68
  205.0 1.9 collective-permute-start.22
  207.0 4.8 %collective-permute-start.20 = (f32[24,64,128]{2,0,1:T(8,128)}, f32[24,64,128]{2,0,1:T(8,128)}, u32[]{:S(2)}, u32[]{:S(2)}) collective-permute-start(f32[24,64,128]{2,0,1:T(8,128)} %collective-permute-done.19), channel_id=1, source_target_pairs={{8,0},{16,8},{24,16},{32,24},{40,32},{48,40},{56,48},{9,1},{17,9},... | collective-permute-start | bytes 2359304 | tf_op jit(solution)/shard_map/ppermute | solution.py:56
  216.5 3.2 %copy.264 = f32[24,64,4,1]{3,0,2,1:T(8,128)} copy(f32[24,64,4,1]{1,0,3,2:T(8,128)} %collective-permute-done.21) | data formatting | bytes 49152 | tf_op jit(solution)/shard_map/ppermute | solution.py:72
  219.7 3.2 %copy.266 = f32[24,64,4,1]{3,0,2,1:T(8,128)} copy(f32[24,64,4,1]{1,0,3,2:T(8,128)} %collective-permute-done.22) | data formatting | bytes 49152 | tf_op jit(solution)/shard_map/ppermute | solution.py:74
  222.9 4.3 %fusion = f32[24,64,4,129]{3,0,2,1:T(8,128)S(1)} fusion(f32[24,64,4,128]{3,0,2,1:T(8,128)S(1)} %fusion.7, f32[24,64,4,1]{3,0,2,1:T(8,128)} %copy.264, f32[24,64,4,1]{3,0,2,1:T(8,128)} %copy.266, f32[64,4,129]{2,1,0:T(4,128)} %copy.288, f32[64,4,129]{2,1,0:T(4,128)S(1)} %copy-done.8), kind=kLoop, calls=%fused_computation.3 | loop fusion | flops 3962880 | bytes 6629376 | tf_op jit(solution)/shard_map/add | solution.py:187
  234.0 1.7 fusion.67
  236.7 4.8 %all-to-all-start.3 = ((f32[64,4,128]{2,1,0:T(4,128)}), f32[64,4,128]{2,1,0:T(4,128)S(1)}, u32[]{:S(2)}, u32[]{:S(2)}) async-start(f32[64,4,128]{2,1,0:T(4,128)} %copy.271), calls=%async_computation.3 | async-start | bytes 262144 | tf_op jit(solution)/shard_map/all_to_all | solution.py:207
  241.7 7.0 %fusion.9 = f32[24,64,1,1,4,128]{5,0,4,1,3,2:T(8,128)S(1)} fusion(f32[24,64,4,128]{3,0,2,1:T(8,128)} %copy-done.2, f32[24]{0:T(128)} %param.24, f32[64,4,128]{2,1,0:T(4,128)S(1)} %copy.275, f32[24]{0:T(128)} %param.23, f32[64,4,128]{2,1,0:T(4,128)S(1)} %bitcast.188, f32[24]{0:T(128)} %param.22, f32[64,4,128]{2,1,0:T(4,128)S(1)} %copy.274, ...), kind=kOutput, calls=%fused_computation.24 | convolution fusion | flops 233570304 | bytes 6687264 | tf_op jit(solution)/shard_map/dot_general | solution.py:215
  248.7 2.5 copy.281
  (161 shorter events, 51.5 us)
Async XLA Ops:
  0.6 241.0 %copy-start = (f32[24,24]{1,0:T(8,128)S(1)}, f32[24,24]{1,0:T(8,128)}, u32[]{:S(2)}) copy-start(f32[24,24]{1,0:T(8,128)} %param.25) | copy-start | bytes 6916
  1.5 32.5 %collective-permute-start.3 = (s32[2,16,1]{2,1,0:T(8,128)S(1)}, s32[2,16,1]{2,1,0:T(8,128)S(1)}, u32[]{:S(2)}, u32[]{:S(2)}) collective-permute-start(s32[2,16,1]{2,1,0:T(8,128)S(1)} %get-tuple-element.77), channel_id=1, source_target_pairs={{1,0},{2,1},{3,2},{4,3},{5,4},{6,5},{7,6},{9,8},{10,9},{11,10},{12... | collective-permute-start | bytes 392 | tf_op jit(solution)/shard_map/ppermute | solution.py:26
  4.1 32.1 %collective-permute-start = (s32[2,16,1]{2,1,0:T(8,128)S(1)}, s32[2,16,1]{2,1,0:T(8,128)S(1)}, u32[]{:S(2)}, u32[]{:S(2)}) collective-permute-start(s32[2,16,1]{2,1,0:T(8,128)S(1)} %get-tuple-element.76), channel_id=1, source_target_pairs={{0,1},{1,2},{2,3},{3,4},{4,5},{5,6},{6,7},{8,9},{9,10},{10,11},{11... | collective-permute-start | bytes 392 | tf_op jit(solution)/shard_map/ppermute | solution.py:25
  9.6 26.6 %collective-permute-start.2 = (s32[2,1,128]{2,1,0:T(1,128)S(1)}, s32[2,1,128]{2,1,0:T(1,128)S(1)}, u32[]{:S(2)}, u32[]{:S(2)}) collective-permute-start(s32[2,1,128]{2,1,0:T(1,128)S(1)} %get-tuple-element.75), channel_id=1, source_target_pairs={{8,0},{16,8},{24,16},{32,24},{40,32},{48,40},{56,48},{9,1},{17,9},... | collective-permute-start | bytes 3080 | tf_op jit(solution)/shard_map/ppermute | solution.py:26
  13.4 22.8 %collective-permute-start.1 = (s32[2,1,128]{2,1,0:T(1,128)S(1)}, s32[2,1,128]{2,1,0:T(1,128)S(1)}, u32[]{:S(2)}, u32[]{:S(2)}) collective-permute-start(s32[2,1,128]{2,1,0:T(1,128)S(1)} %get-tuple-element.74), channel_id=1, source_target_pairs={{0,8},{8,16},{16,24},{24,32},{32,40},{40,48},{48,56},{1,9},{9,17},... | collective-permute-start | bytes 3080 | tf_op jit(solution)/shard_map/ppermute | solution.py:25
  22.7 7.6 %copy-start.32 = (s32[16,128]{1,0:T(8,128)S(1)}, s32[16,128]{1,0:T(8,128)}, u32[]{:S(2)}) copy-start(s32[16,128]{1,0:T(8,128)} %param.18) | copy-start | bytes 24580
  22.7 7.6 %copy-start.31 = (s32[16,128]{1,0:T(8,128)S(1)}, s32[16,128]{1,0:T(8,128)}, u32[]{:S(2)}) copy-start(s32[16,128]{1,0:T(8,128)} %param.17) | copy-start | bytes 24580
  25.9 58.8 %collective-permute-start.15 = (f32[24,64,4,1]{1,0,3,2:T(8,128)}, f32[24,64,4,1]{1,0,3,2:T(8,128)}, u32[]{:S(2)}, u32[]{:S(2)}) collective-permute-start(f32[24,64,4,1]{1,0,3,2:T(8,128)} %copy.252), channel_id=1, source_target_pairs={{0,1},{1,2},{2,3},{3,4},{4,5},{5,6},{6,7},{8,9},{9,10},{10,11},{11... | collective-permute-start | bytes 73736 | tf_op jit(solution)/shard_map/ppermute | solution.py:72
  28.5 8.7 %copy-start.30 = (f32[16,16,128]{2,1,0:T(8,128)S(1)}, f32[16,16,128]{2,1,0:T(8,128)}, u32[]{:S(2)}) copy-start(f32[16,16,128]{2,1,0:T(8,128)} %param.16) | copy-start | bytes 393220
  34.0 53.6 %collective-permute-start.16 = (f32[24,64,4,1]{1,0,3,2:T(8,128)}, f32[24,64,4,1]{1,0,3,2:T(8,128)}, u32[]{:S(2)}, u32[]{:S(2)}) collective-permute-start(f32[24,64,4,1]{1,0,3,2:T(8,128)} %copy.255), channel_id=1, source_target_pairs={{1,0},{2,1},{3,2},{4,3},{5,4},{6,5},{7,6},{9,8},{10,9},{11,10},{12... | collective-permute-start | bytes 73736 | tf_op jit(solution)/shard_map/ppermute | solution.py:74
  39.5 7.5 %all-to-all-start = ((f32[4,1,16,128]{3,2,1,0:T(8,128)}), f32[4,1,16,128]{3,2,1,0:T(8,128)S(1)}, u32[]{:S(2)}, u32[]{:S(2)}) async-start(f32[4,1,16,128]{3,2,1,0:T(8,128)} %broadcast_in_dim.10), calls=%async_computation | async-start | bytes 65536 | tf_op jit(solution)/shard_map/all_to_all | solution.py:39
  47.0 11.9 %copy-start.5 = (f32[16,18,130]{2,0,1:T(8,128)S(1)}, f32[16,18,130]{2,0,1:T(8,128)}, u32[]{:S(2)}) copy-start(f32[16,18,130]{2,0,1:T(8,128)} %copy-done.4) | copy-start | bytes 449284
  47.0 20.7 %copy-start.12 = (f32[16,16,129]{2,0,1:T(8,128)S(1)}, f32[16,16,129]{2,0,1:T(8,128)}, u32[]{:S(2)}) copy-start(f32[16,16,129]{2,0,1:T(8,128)} %slice_multiply_fusion) | copy-start | bytes 396292
  50.0 15.1 %collective-permute-start.6 = (f32[3,16,16,1]{3,1,2,0:T(8,128)S(1)}, f32[3,16,16,1]{3,1,2,0:T(8,128)S(1)}, u32[]{:S(2)}, u32[]{:S(2)}) collective-permute-start(f32[3,16,16,1]{3,1,2,0:T(8,128)S(1)} %get-tuple-element.57), channel_id=1, source_target_pairs={{1,0},{2,1},{3,2},{4,3},{5,4},{6,5},{7,6},{9,8},{10,9},{11,10},{12... | collective-permute-start | bytes 9224 | tf_op jit(solution)/shard_map/ppermute | solution.py:26
  52.7 14.0 %collective-permute-start.4 = (f32[3,16,1,128]{3,1,2,0:T(8,128)S(1)}, f32[3,16,1,128]{3,1,2,0:T(8,128)S(1)}, u32[]{:S(2)}, u32[]{:S(2)}) collective-permute-start(f32[3,16,1,128]{3,1,2,0:T(8,128)S(1)} %get-tuple-element.61), channel_id=1, source_target_pairs={{8,0},{16,8},{24,16},{32,24},{40,32},{48,40},{56,48},{9,1},{17,9},... | collective-permute-start | bytes 73736 | tf_op jit(solution)/shard_map/ppermute | solution.py:26
  57.0 9.7 %collective-permute-start.5 = (f32[3,16,1,128]{3,1,2,0:T(8,128)S(1)}, f32[3,16,1,128]{3,1,2,0:T(8,128)S(1)}, u32[]{:S(2)}, u32[]{:S(2)}) collective-permute-start(f32[3,16,1,128]{3,1,2,0:T(8,128)S(1)} %get-tuple-element.60), channel_id=1, source_target_pairs={{0,8},{8,16},{16,24},{24,32},{32,40},{40,48},{48,56},{1,9},{9,17},... | collective-permute-start | bytes 73736 | tf_op jit(solution)/shard_map/ppermute | solution.py:25
  59.1 10.5 %copy-start.18 = (f32[16,17,128]{2,0,1:T(8,128)}, f32[16,17,128]{2,0,1:T(8,128)S(1)}, u32[]{:S(2)}) copy-start(f32[16,17,128]{2,0,1:T(8,128)S(1)} %slice_multiply_fusion.1) | copy-start | bytes 417796
  65.1 48.8 %collective-permute-start.12 = (f32[24,64,128]{2,0,1:T(8,128)}, f32[24,64,128]{2,0,1:T(8,128)}, u32[]{:S(2)}, u32[]{:S(2)}) collective-permute-start(f32[24,64,128]{2,0,1:T(8,128)} %get-tuple-element.51), channel_id=1, source_target_pairs={{0,192},{64,0},{128,64},{192,128},{1,193},{65,1},{129,65},{193,129... | collective-permute-start | bytes 2359304 | tf_op jit(solution)/shard_map/ppermute | solution.py:61
  66.7 3.5 %copy-start.26 = (f32[3,16,1,128]{3,1,2,0:T(8,128)}, f32[3,16,1,128]{3,1,2,0:T(8,128)S(1)}, u32[]{:S(2)}) copy-start(f32[3,16,1,128]{3,1,2,0:T(8,128)S(1)} %collective-permute-done.4) | copy-start | bytes 73732
  66.7 51.5 %collective-permute-start.10 = (f32[24,64,128]{2,0,1:T(8,128)}, f32[24,64,128]{2,0,1:T(8,128)}, u32[]{:S(2)}, u32[]{:S(2)}) collective-permute-start(f32[24,64,128]{2,0,1:T(8,128)} %get-tuple-element.50), channel_id=1, source_target_pairs={{0,64},{64,128},{128,192},{192,0},{1,65},{65,129},{129,193},{193,1... | collective-permute-start | bytes 2359304 | tf_op jit(solution)/shard_map/ppermute | solution.py:61
  66.7 3.5 %copy-start.28 = (f32[3,16,1,128]{3,1,2,0:T(8,128)}, f32[3,16,1,128]{3,1,2,0:T(8,128)S(1)}, u32[]{:S(2)}) copy-start(f32[3,16,1,128]{3,1,2,0:T(8,128)S(1)} %collective-permute-done.5) | copy-start | bytes 73732
  70.9 19.7 %all-to-all-start.2 = ((f32[4,16,4,128]{3,1,2,0:T(8,128)}), f32[4,16,4,128]{3,1,2,0:T(8,128)}, u32[]{:S(2)}, u32[]{:S(2)}) async-start(f32[4,16,4,128]{3,1,2,0:T(8,128)} %pad_maximum_fusion.14), calls=%async_computation.2 | async-start | bytes 262144 | tf_op jit(solution)/shard_map/all_to_all | solution.py:140
  90.6 9.9 %all-to-all-start.1 = ((f32[16,16,128]{2,0,1:T(8,128)}), f32[16,16,128]{2,0,1:T(8,128)}, u32[]{:S(2)}, u32[]{:S(2)}) async-start(f32[16,16,128]{2,0,1:T(8,128)} %get-tuple-element.59), calls=%async_computation.1 | async-start | bytes 262144 | tf_op jit(solution)/shard_map/all_to_all | solution.py:138
  97.2 6.7 %collective-permute-start.14 = (f32[64,4]{0,1:T(4,128)}, f32[64,4]{0,1:T(4,128)}, u32[]{:S(2)}, u32[]{:S(2)}) collective-permute-start(f32[64,4]{0,1:T(4,128)} %slice_reduce_fusion), channel_id=1, source_target_pairs={{0,1},{1,2},{2,3},{3,4},{4,5},{5,6},{6,7},{8,9},{9,10},{10,11},{11... | collective-permute-start | bytes 3080 | tf_op jit(solution)/shard_map/ppermute | solution.py:56
  102.7 9.3 %collective-permute-start.8 = (f32[64,128]{1,0:T(8,128)}, f32[64,128]{1,0:T(8,128)}, u32[]{:S(2)}, u32[]{:S(2)}) collective-permute-start(f32[64,128]{1,0:T(8,128)} %slice_bitcast_fusion.11), channel_id=1, source_target_pairs={{0,64},{64,128},{128,192},{192,0},{1,65},{65,129},{129,193},{193,1... | collective-permute-start | bytes 98312 | tf_op jit(solution)/shard_map/ppermute | solution.py:61
  106.4 4.7 %copy-start.9 = (f32[64,4,129]{2,0,1:T(8,128)}, f32[64,4,129]{2,0,1:T(8,128)S(1)}, u32[]{:S(2)}) copy-start(f32[64,4,129]{2,0,1:T(8,128)S(1)} %get-tuple-element.65) | copy-start | bytes 396292
  112.0 12.7 %collective-permute-start.9 = (f32[64,128]{1,0:T(8,128)}, f32[64,128]{1,0:T(8,128)S(1)}, u32[]{:S(2)}, u32[]{:S(2)}) collective-permute-start(f32[64,128]{1,0:T(8,128)} %collective-permute-done.8), channel_id=1, source_target_pairs={{0,8},{8,16},{16,24},{24,32},{32,40},{40,48},{48,56},{1,9},{9,17},... | collective-permute-start | bytes 98312 | tf_op jit(solution)/shard_map/ppermute | solution.py:56
  113.9 40.0 %collective-permute-start.13 = (f32[24,64,128]{2,0,1:T(8,128)}, f32[24,64,128]{2,0,1:T(8,128)}, u32[]{:S(2)}, u32[]{:S(2)}) collective-permute-start(f32[24,64,128]{2,0,1:T(8,128)} %collective-permute-done.12), channel_id=1, source_target_pairs={{8,0},{16,8},{24,16},{32,24},{40,32},{48,40},{56,48},{9,1},{17,9},... | collective-permute-start | bytes 2359304 | tf_op jit(solution)/shard_map/ppermute | solution.py:56
  118.2 34.5 %collective-permute-start.11 = (f32[24,64,128]{2,0,1:T(8,128)}, f32[24,64,128]{2,0,1:T(8,128)}, u32[]{:S(2)}, u32[]{:S(2)}) collective-permute-start(f32[24,64,128]{2,0,1:T(8,128)} %collective-permute-done.10), channel_id=1, source_target_pairs={{0,8},{8,16},{16,24},{24,32},{32,40},{40,48},{48,56},{1,9},{9,17},... | collective-permute-start | bytes 2359304 | tf_op jit(solution)/shard_map/ppermute | solution.py:56
  124.7 30.5 %copy-start.3 = (f32[24,64,1,1,4,128]{5,0,4,1,2,3:T(8,128)S(1)}, f32[24,64,1,1,4,128]{5,0,4,1,2,3:T(8,128)}, u32[]{:S(2)}) copy-start(f32[24,64,1,1,4,128]{5,0,4,1,2,3:T(8,128)} %copy.346) | copy-start | bytes 9437188
  126.6 28.6 %copy-start.16 = (f32[64,5,128]{2,0,1:T(8,128)}, f32[64,5,128]{2,0,1:T(8,128)S(1)}, u32[]{:S(2)}) copy-start(f32[64,5,128]{2,0,1:T(8,128)S(1)} %get-tuple-element.67) | copy-start | bytes 491524
  163.9 15.2 %copy-start.7 = (f32[3,16,18,129]{3,1,2,0:T(8,128)S(1)}, f32[3,16,18,129]{3,1,2,0:T(8,128)}, u32[]{:S(2)}) copy-start(f32[3,16,18,129]{3,1,2,0:T(8,128)} %copy-done.6) | copy-start | bytes 1337476
  163.9 15.2 %copy-start.13 = (f32[16,16,129]{2,0,1:T(8,128)S(1)}, f32[16,16,129]{2,0,1:T(8,128)}, u32[]{:S(2)}) copy-start(f32[16,16,129]{2,0,1:T(8,128)} %slice_multiply_fusion) | copy-start | bytes 396292
  163.9 15.2 %copy-start.27 = (f32[3,16,1,128]{3,1,2,0:T(8,128)S(1)}, f32[3,16,1,128]{3,1,2,0:T(8,128)}, u32[]{:S(2)}) copy-start(f32[3,16,1,128]{3,1,2,0:T(8,128)} %copy-done.26) | copy-start | bytes 73732
  163.9 15.2 %copy-start.29 = (f32[3,16,1,128]{3,1,2,0:T(8,128)S(1)}, f32[3,16,1,128]{3,1,2,0:T(8,128)}, u32[]{:S(2)}) copy-start(f32[3,16,1,128]{3,1,2,0:T(8,128)} %copy-done.28) | copy-start | bytes 73732
  163.9 16.1 %copy-start.19 = (f32[16,17,128]{2,0,1:T(8,128)S(1)}, f32[16,17,128]{2,0,1:T(8,128)}, u32[]{:S(2)}) copy-start(f32[16,17,128]{2,0,1:T(8,128)} %copy-done.18) | copy-start | bytes 417796
  164.9 18.1 %collective-permute-start.17 = (f32[24,64,128]{2,0,1:T(8,128)S(1)}, f32[24,64,128]{2,0,1:T(8,128)}, u32[]{:S(2)}, u32[]{:S(2)}) collective-permute-start(f32[24,64,128]{2,0,1:T(8,128)S(1)} %get-tuple-element.47), channel_id=1, source_target_pairs={{0,64},{64,128},{128,192},{192,0},{1,65},{65,129},{129,193},{193,1... | collective-permute-start | bytes 2359304 | tf_op jit(solution)/shard_map/ppermute | solution.py:61
  165.8 13.3 %collective-permute-start.7 = (f32[3,16,16,1]{3,1,2,0:T(8,128)S(1)}, f32[3,16,16,1]{3,1,2,0:T(8,128)S(1)}, u32[]{:S(2)}, u32[]{:S(2)}) collective-permute-start(f32[3,16,16,1]{3,1,2,0:T(8,128)S(1)} %copy-done.25), channel_id=1, source_target_pairs={{0,1},{1,2},{2,3},{3,4},{4,5},{5,6},{6,7},{8,9},{9,10},{10,11},{11... | collective-permute-start | bytes 9224 | tf_op jit(solution)/shard_map/ppermute | solution.py:25
  179.4 27.6 %collective-permute-start.19 = (f32[24,64,128]{2,0,1:T(8,128)}, f32[24,64,128]{2,0,1:T(8,128)}, u32[]{:S(2)}, u32[]{:S(2)}) collective-permute-start(f32[24,64,128]{2,0,1:T(8,128)} %get-tuple-element.46), channel_id=1, source_target_pairs={{0,192},{64,0},{128,64},{192,128},{1,193},{65,1},{129,65},{193,129... | collective-permute-start | bytes 2359304 | tf_op jit(solution)/shard_map/ppermute | solution.py:61
  183.0 44.2 %collective-permute-start.18 = (f32[24,64,128]{2,0,1:T(8,128)}, f32[24,64,128]{2,0,1:T(8,128)}, u32[]{:S(2)}, u32[]{:S(2)}) collective-permute-start(f32[24,64,128]{2,0,1:T(8,128)} %collective-permute-done.17), channel_id=1, source_target_pairs={{0,8},{8,16},{16,24},{24,32},{32,40},{40,48},{48,56},{1,9},{9,17},... | collective-permute-start | bytes 2359304 | tf_op jit(solution)/shard_map/ppermute | solution.py:56
  190.2 24.1 %copy-start.22 = (f32[16,16,128]{2,0,1:T(8,128)S(1)}, f32[16,16,128]{2,0,1:T(8,128)}, u32[]{:S(2)}) copy-start(f32[16,16,128]{2,0,1:T(8,128)} %copy-done.21) | copy-start | bytes 393220
  190.2 25.4 %copy-start.10 = (f32[64,4,129]{2,0,1:T(8,128)S(1)}, f32[64,4,129]{2,0,1:T(8,128)}, u32[]{:S(2)}) copy-start(f32[64,4,129]{2,0,1:T(8,128)} %copy-done.9) | copy-start | bytes 396292
  193.5 23.0 %collective-permute-start.21 = (f32[24,64,4,1]{1,0,3,2:T(8,128)}, f32[24,64,4,1]{1,0,3,2:T(8,128)}, u32[]{:S(2)}, u32[]{:S(2)}) collective-permute-start(f32[24,64,4,1]{1,0,3,2:T(8,128)} %copy.263), channel_id=1, source_target_pairs={{0,1},{1,2},{2,3},{3,4},{4,5},{5,6},{6,7},{8,9},{9,10},{10,11},{11... | collective-permute-start | bytes 73736 | tf_op jit(solution)/shard_map/ppermute | solution.py:72
  205.0 14.7 %collective-permute-start.22 = (f32[24,64,4,1]{1,0,3,2:T(8,128)}, f32[24,64,4,1]{1,0,3,2:T(8,128)}, u32[]{:S(2)}, u32[]{:S(2)}) collective-permute-start(f32[24,64,4,1]{1,0,3,2:T(8,128)} %copy.265), channel_id=1, source_target_pairs={{1,0},{2,1},{3,2},{4,3},{5,4},{6,5},{7,6},{9,8},{10,9},{11,10},{12... | collective-permute-start | bytes 73736 | tf_op jit(solution)/shard_map/ppermute | solution.py:74
  207.0 21.6 %collective-permute-start.20 = (f32[24,64,128]{2,0,1:T(8,128)}, f32[24,64,128]{2,0,1:T(8,128)}, u32[]{:S(2)}, u32[]{:S(2)}) collective-permute-start(f32[24,64,128]{2,0,1:T(8,128)} %collective-permute-done.19), channel_id=1, source_target_pairs={{8,0},{16,8},{24,16},{32,24},{40,32},{48,40},{56,48},{9,1},{17,9},... | collective-permute-start | bytes 2359304 | tf_op jit(solution)/shard_map/ppermute | solution.py:56
  216.5 6.4 %copy-start.8 = (f32[64,4,129]{2,1,0:T(4,128)S(1)}, f32[64,4,129]{2,1,0:T(4,128)}, u32[]{:S(2)}) copy-start(f32[64,4,129]{2,1,0:T(4,128)} %copy.251) | copy-start | bytes 396292
  232.3 3.4 %copy-start.33 = (pred[4,128]{1,0:T(4,128)(4,1)S(1)}, pred[4,128]{1,0:T(4,128)(4,1)}, u32[]{:S(2)}) copy-start(pred[4,128]{1,0:T(4,128)(4,1)} %dynamic-slice_compare_fusion) | copy-start | bytes 1540
  236.7 14.5 %all-to-all-start.3 = ((f32[64,4,128]{2,1,0:T(4,128)}), f32[64,4,128]{2,1,0:T(4,128)S(1)}, u32[]{:S(2)}, u32[]{:S(2)}) async-start(f32[64,4,128]{2,1,0:T(4,128)} %copy.271), calls=%async_computation.3 | async-start | bytes 262144 | tf_op jit(solution)/shard_map/all_to_all | solution.py:207
  (15 other events, 24.9 us)
